TPU v7x, 128 devices: a whole 4x4x4 slice. The times are simulated.
128 devices in a mesh: pair: 2 (over core), batch: 4 (over y), vocab: 16 (over x, z).
Axes of the slice: x: 4, y: 4, z: 4, core: 2. Of those that a mesh axis runs over, the one named last changes fastest.
Arguments:
- hidden: bfloat16 [2, 512, 8192], P('pair', 'batch', 'vocab'), may hold values from -120 to 120
- norm_gain: bfloat16 [8192], P('vocab'), may hold values from 0.099609375 to 1.8984375
- head_weight: bfloat16 [8192, 65536], P(('pair', 'batch'), 'vocab'), may hold values from -1 to 1
Outputs:
- guided_logprobs: float32 [512, 65536], P(('pair', 'batch'), 'vocab')
- cond_logprobs: float32 [512, 65536], P(('pair', 'batch'), 'vocab')
All inputs are finite; a program needn't handle non-finite values.
Results may differ from a plain program's by a relative error of at most 0.007.
Values may be sent and summed in bfloat16 or wider, within the bound.
A program may use at most 128 MiB of HBM per device.

v0:
```python
import jax
import jax.numpy as jnp
from jax import lax
from jax.sharding import PartitionSpec as P

D = 8192
EPS = 1e-05
GUIDE = 1.5
CHUNKS = 2


def on_device(hidden, norm_gain, head_weight):
    local_rows = hidden.shape[1]
    pad = jnp.zeros((15, norm_gain.shape[0]), hidden.dtype)
    packed = jnp.concatenate([hidden[0], norm_gain[None, :], pad], axis=0)
    gathered = lax.all_gather(packed, "vocab", axis=1, tiled=True)
    wide = gathered[:local_rows].astype(jnp.float32)
    gain = gathered[local_rows]
    total_sq = jnp.sum(wide * wide, axis=1)
    scaled = wide * lax.rsqrt(total_sq / D + EPS)[:, None] * gain.astype(jnp.float32)[None, :]
    features = scaled.astype(jnp.bfloat16)
    blocks = lax.all_to_all(features, ("pair", "batch"), split_axis=1, concat_axis=0, tiled=True)
    groups = lax.axis_size("pair") * lax.axis_size("batch")
    width = blocks.shape[1]
    out_rows = blocks.shape[0] // (2 * groups)
    ordered = blocks.reshape(2, groups, out_rows, width).transpose(1, 0, 2, 3).reshape(-1, width)
    half_rows = ordered.shape[0] // 2
    me = lax.axis_index("pair")
    mine = lax.dynamic_slice_in_dim(ordered, me * half_rows, half_rows, axis=0)
    theirs = lax.dynamic_slice_in_dim(ordered, (1 - me) * half_rows, half_rows, axis=0)
    cols = head_weight.shape[1]
    step = cols // CHUNKS
    pieces = []
    for j in range(CHUNKS):
        w = head_weight[:, j * step : (j + 1) * step]
        sent = jnp.dot(theirs, w, preferred_element_type=jnp.float32)
        got = lax.ppermute(sent, "pair", [(0, 1), (1, 0)])
        kept = jnp.dot(mine, w, preferred_element_type=jnp.float32)
        pieces.append(lax.psum_scatter(kept + got, "batch", scatter_dimension=0, tiled=True))
    logits = jnp.concatenate(pieces, axis=1)
    cond = logits[:out_rows]
    uncond = logits[out_rows:]
    guided = GUIDE * cond + (1.0 - GUIDE) * uncond
    peak_c = jnp.max(cond, axis=1)
    peak_g = jnp.max(guided, axis=1)
    local_c = jnp.sum(jnp.exp(cond - peak_c[:, None]), axis=1)
    local_g = jnp.sum(jnp.exp(guided - peak_g[:, None]), axis=1)
    stats = jnp.stack([peak_c, local_c, peak_g, local_g])
    every = lax.all_gather(stats, "vocab", axis=0)
    top_c = jnp.max(every[:, 0], axis=0)
    top_g = jnp.max(every[:, 2], axis=0)
    total_c = jnp.sum(every[:, 1] * jnp.exp(every[:, 0] - top_c[None, :]), axis=0)
    total_g = jnp.sum(every[:, 3] * jnp.exp(every[:, 2] - top_g[None, :]), axis=0)
    cond_out = cond - (top_c + jnp.log(total_c))[:, None]
    guided_out = guided - (top_g + jnp.log(total_g))[:, None]
    return (guided_out, cond_out)


def solution(mesh):
    in_specs = (P("pair", "batch", "vocab"), P("vocab"), P(("pair", "batch"), "vocab"))
    out_specs = (P(("pair", "batch"), "vocab"), P(("pair", "batch"), "vocab"))
    return jax.shard_map(
        on_device, mesh=mesh, in_specs=in_specs, out_specs=out_specs, check_vma=False
    )
```

profile of v0, /device:TPU:0, one launch (start us, length us, event | category | flops | bytes accessed | tf_op | source)
XLA Modules:
  0.0 259.7 jit_solution(1291108250158917924)
XLA Ops:
  7.2 0.0 all-gather.4.cloned.1.call-start
  7.2 1.0 copy.21
  8.2 0.8 broadcast_in_dim.6
  9.1 0.1 pad.6.clone
  9.1 0.8 maximum_maximum_fusion
  9.9 0.0 all-gather.4.cloned.1.call-update
  9.9 54.9 %all-gather.4.cloned.1.call-done = bf16[144,8192]{0,1:T(8,128)(2,1)} async-done(((bf16[144,512]{0,1:T(8,128)(2,1)}), bf16[144,8192]{0,1:T(8,128)(2,1)}) %all-gather.4.cloned.1.call-update) | async-done | bytes 2359312 | tf_op jit(solution)/shard_map/all_gather | solution.py:16
  64.9 0.0 copy-start
  64.9 2.8 %fusion = f32[128]{0:T(128)S(1)} fusion(bf16[144,8192]{0,1:T(8,128)(2,1)} %all-gather.4.cloned.1.call-done), kind=kLoop, calls=%fused_computation.2 | loop fusion | flops 3145600 | bytes 2097664 | tf_op jit(solution)/shard_map/reduce_sum | solution.py:19
  67.7 2.2 convert_reduce_fusion
  70.0 0.0 copy-done
  70.0 4.4 %fusion.2 = bf16[128,8192]{0,1:T(8,128)(2,1)} fusion(f32[8192]{0:T(1024)S(1)} %convert_reduce_fusion, f32[128]{0:T(128)S(1)} %add_rsqrt_fusion, bf16[144,8192]{0,1:T(8,128)(2,1)S(1)} %copy-done), kind=kLoop, calls=%fused_computation.4 | loop fusion | flops 4194304 | bytes 4227584 | tf_op jit(solution)/shard_map/convert_element_type | solution.py:21
  74.4 4.3 %all-to-all-start = ((bf16[128,8,1024]{0,2,1:T(8,128)(2,1)}), bf16[128,8,1024]{0,2,1:T(8,128)(2,1)S(1)}, u32[]{:S(2)}, u32[]{:S(2)}) async-start(bf16[128,8,1024]{0,2,1:T(8,128)(2,1)} %bitcast.22), calls=%async_computation | async-start | bytes 4194304 | tf_op jit(solution)/shard_map/all_to_all | solution.py:22
  78.6 0.0 reduce-scatter.3.cloned.1.call-start
  78.7 26.5 %all-to-all-done = bf16[128,8,1024]{0,2,1:T(8,128)(2,1)S(1)} async-done(((bf16[128,8,1024]{0,2,1:T(8,128)(2,1)}), bf16[128,8,1024]{0,2,1:T(8,128)(2,1)S(1)}, u32[]{:S(2)}, u32[]{:S(2)}) %all-to-all-start) | async-done | bytes 2097184 | tf_op jit(solution)/shard_map/all_to_all | solution.py:22
  105.2 2.6 %copy.23 = bf16[8,128,1024]{2,1,0:T(8,128)(2,1)} copy(bf16[8,128,1024]{1,2,0:T(8,128)(2,1)S(1)} %bitcast.21) | data formatting | bytes 4194304 | tf_op jit(solution)/shard_map/all_to_all | solution.py:22
  107.8 1.8 copy.24
  109.7 6.5 %fusion.7 = f32[512,2048]{1,0:T(8,128)} fusion(bf16[1024,4096]{1,0:T(8,128)(2,1)} %param.5, bf16[1024,1024]{1,0:T(8,128)(2,1)S(1)} %bitcast.24, s32[]{:T(128)S(6)} %select_n.7), kind=kOutput, calls=%fused_computation.10 | convolution fusion | flops 2147483648 | bytes 9437188 | tf_op jit(solution)/shard_map/dot_general | solution.py:36
  116.1 0.1 collective-permute-start
  116.3 7.4 %collective-permute-done = f32[512,2048]{1,0:T(8,128)} collective-permute-done((f32[512,2048]{1,0:T(8,128)}, f32[512,2048]{1,0:T(8,128)}, u32[]{:S(2)}, u32[]{:S(2)}) %collective-permute-start) | collective-permute-done | bytes 4194336 | tf_op jit(solution)/shard_map/ppermute | solution.py:37
  123.6 7.7 %fusion.11 = f32[512,2048]{1,0:T(8,128)} fusion(f32[512,2048]{1,0:T(8,128)} %collective-permute-done, bf16[1024,4096]{1,0:T(8,128)(2,1)} %param.5, bf16[1024,1024]{1,0:T(8,128)(2,1)S(1)} %bitcast.25, s32[]{:T(128)S(6)} %select_n.6), kind=kOutput, calls=%fused_computation.14 | convolution fusion | flops 2148532224 | bytes 13631492 | tf_op jit(solution)/shard_map/dot_general | solution.py:38
  131.4 0.0 reduce-scatter.3.cloned.1.call-update
  131.4 0.0 reduce-scatter.5.cloned.1.call-start
  131.4 4.5 %fusion.3 = f32[512,2048]{1,0:T(8,128)S(1)} fusion(bf16[1024,4096]{1,0:T(8,128)(2,1)} %param.5, bf16[1024,1024]{1,0:T(8,128)(2,1)S(1)} %bitcast.26, s32[]{:T(128)S(6)} %select_n.7), kind=kOutput, calls=%fused_computation.6 | convolution fusion | flops 2147483648 | bytes 9437188 | tf_op jit(solution)/shard_map/dot_general | solution.py:36
  136.0 0.4 collective-permute-start.1
  136.4 7.0 %collective-permute-done.1 = f32[512,2048]{1,0:T(8,128)S(1)} collective-permute-done((f32[512,2048]{1,0:T(8,128)S(1)}, f32[512,2048]{1,0:T(8,128)S(1)}, u32[]{:S(2)}, u32[]{:S(2)}) %collective-permute-start.1) | collective-permute-done | bytes 4194336 | tf_op jit(solution)/shard_map/ppermute | solution.py:37
  143.4 6.5 %fusion.14 = f32[512,2048]{1,0:T(8,128)} fusion(f32[512,2048]{1,0:T(8,128)S(1)} %collective-permute-done.1, bf16[1024,4096]{1,0:T(8,128)(2,1)} %param.5, bf16[1024,1024]{1,0:T(8,128)(2,1)S(1)} %bitcast.27, s32[]{:T(128)S(6)} %select_n.6), kind=kOutput, calls=%fused_computation.15 | convolution fusion | flops 2148532224 | bytes 13631492 | tf_op jit(solution)/shard_map/dot_general | solution.py:38
  149.9 0.0 reduce-scatter.5.cloned.1.call-update
  149.9 26.8 %reduce-scatter.3.cloned.1.call-done = f32[128,2048]{1,0:T(8,128)} async-done(((f32[512,2048]{1,0:T(8,128)}), f32[128,2048]{1,0:T(8,128)}) %reduce-scatter.3.cloned.1.call-update) | async-done | bytes 1048592 | tf_op jit(solution)/shard_map/reduce_scatter | solution.py:39
  176.7 1.3 constant_dynamic-update-slice_fusion.1
  178.0 47.8 %reduce-scatter.5.cloned.1.call-done = f32[128,2048]{1,0:T(8,128)} async-done(((f32[512,2048]{1,0:T(8,128)}), f32[128,2048]{1,0:T(8,128)}) %reduce-scatter.5.cloned.1.call-update) | async-done | bytes 1048592 | tf_op jit(solution)/shard_map/reduce_scatter | solution.py:39
  225.8 1.3 constant_dynamic-update-slice_fusion
  227.1 0.3 slice_reduce_fusion
  227.4 0.5 exponential_reduce_fusion.1
  228.0 23.5 %all-gather.1 = f32[16,4,64]{2,1,0:T(4,128)S(1)} all-gather(f32[1,4,64]{2,1,0:T(4,128)S(1)} %maximum_bitcast_fusion), channel_id=2, replica_groups=mesh['pair'=2,'batch'=4,'vocab'=16] {'vocab'}, dimensions={0}, use_global_device_ids=true | all-gather | bytes 17408 | tf_op jit(solution)/shard_map/all_gather | solution.py:49
  251.6 1.6 slice_subtract_fusion
  (8 shorter events, 0.1 us)
Async XLA Ops:
  7.2 57.7 %all-gather.4.cloned.1.call-start = ((), (), s32[]{:S(2)}) async-start(), calls=%async_computation.3 | async-start | bytes 4456448 | tf_op jit(solution)/shard_map/all_gather | solution.py:16
  64.9 5.1 %copy-start = (bf16[144,8192]{0,1:T(8,128)(2,1)S(1)}, bf16[144,8192]{0,1:T(8,128)(2,1)}, u32[]{:S(2)}) copy-start(bf16[144,8192]{0,1:T(8,128)(2,1)} %all-gather.4.cloned.1.call-done) | copy-start | bytes 7077892
  74.4 30.9 %all-to-all-start = ((bf16[128,8,1024]{0,2,1:T(8,128)(2,1)}), bf16[128,8,1024]{0,2,1:T(8,128)(2,1)S(1)}, u32[]{:S(2)}, u32[]{:S(2)}) async-start(bf16[128,8,1024]{0,2,1:T(8,128)(2,1)} %bitcast.22), calls=%async_computation | async-start | bytes 4194304 | tf_op jit(solution)/shard_map/all_to_all | solution.py:22
  78.6 98.1 %reduce-scatter.3.cloned.1.call-start = ((), (), s32[]{:S(2)}) async-start(), calls=%async_computation.4 | async-start | bytes 5242880 | tf_op jit(solution)/shard_map/reduce_scatter | solution.py:39
  116.1 7.5 %collective-permute-start = (f32[512,2048]{1,0:T(8,128)}, f32[512,2048]{1,0:T(8,128)}, u32[]{:S(2)}, u32[]{:S(2)}) collective-permute-start(f32[512,2048]{1,0:T(8,128)} %fusion.7), channel_id=1, source_target_pairs={{0,64},{64,0},{1,65},{65,1},{2,66},{66,2},{3,67},{67,3},{4,68},{68... | collective-permute-start | bytes 12582920 | tf_op jit(solution)/shard_map/ppermute | solution.py:37
  131.4 94.4 %reduce-scatter.5.cloned.1.call-start = ((), (), s32[]{:S(2)}) async-start(), calls=%async_computation.5 | async-start | bytes 5242880 | tf_op jit(solution)/shard_map/reduce_scatter | solution.py:39
  136.0 7.4 %collective-permute-start.1 = (f32[512,2048]{1,0:T(8,128)S(1)}, f32[512,2048]{1,0:T(8,128)S(1)}, u32[]{:S(2)}, u32[]{:S(2)}) collective-permute-start(f32[512,2048]{1,0:T(8,128)S(1)} %fusion.3), channel_id=1, source_target_pairs={{0,64},{64,0},{1,65},{65,1},{2,66},{66,2},{3,67},{67,3},{4,68},{68... | collective-permute-start | bytes 12582920 | tf_op jit(solution)/shard_map/ppermute | solution.py:37
Sparse Core Ops, SparseCore 0:
  10.7 54.1 all-gather.3
  131.5 45.1 reduce-scatter.2
  179.3 46.5 reduce-scatter.4
where the time goes:
time: 260 us
  waiting for transfers between devices  170 us (65%)
  matrix products  25.2 us (10%)
  blocking collectives  23.5 us (9%)
  between operations  13.8 us (5%)
  other arithmetic  12.8 us (5%)
  local copies, waits for them, and re-layouts  8.95 us (3%)
  starting transfers between devices  4.96 us (2%)
    reduce_scatter x2, waiting for transfers between devices, on_device(): lax.psum_scatter(kept + got, 'batch', scatter_dimension=0, tiled=True)  74.6 us
    all_gather x1, waiting for transfers between devices, on_device(): gathered = lax.all_gather(packed, 'vocab', axis=1, tiled=True)  54.9 us
    all_to_all x1, waiting for transfers between devices, on_device(): lax.all_to_all(features, ('pair', 'batch'), split_axis=1, concat_axis=0,...  26.5 us
    all_gather x1, blocking collectives, on_device(): every = lax.all_gather(stats, 'vocab', axis=0)  23.5 us
    ppermute x2, waiting for transfers between devices, on_device(): got = lax.ppermute(sent, 'pair', [(0, 1), (1, 0)])  14.4 us
    dot_general x2, matrix products, on_device(): kept = jnp.dot(mine, w, preferred_element_type=jnp.float32)  14.2 us
    dot_general x2, matrix products, on_device(): sent = jnp.dot(theirs, w, preferred_element_type=jnp.float32)  11 us
  transfers between devices with their start and end apart: 6, of which 6 were waited for; matrix products, arithmetic and copies ran while one was open for 5% of the time, Pallas kernels for 0%

commit v1 on v0

--- a/solution.py
+++ b/solution.py
@@ -19,7 +19,19 @@
     total_sq = jnp.sum(wide * wide, axis=1)
     scaled = wide * lax.rsqrt(total_sq / D + EPS)[:, None] * gain.astype(jnp.float32)[None, :]
     features = scaled.astype(jnp.bfloat16)
-    blocks = lax.all_to_all(features, ("pair", "batch"), split_axis=1, concat_axis=0, tiled=True)
+    ways, here = (lax.axis_size(("pair", "batch")), lax.axis_index(("pair", "batch")))
+    width_2 = features.shape[1] // ways
+    dims = list(features.shape)
+    dims[1] = width_2
+    height = dims[0]
+    dims[0] = height * ways
+    full = jnp.zeros(dims, features.dtype)
+    for mask in range(ways):
+        part = lax.dynamic_slice_in_dim(features, (here ^ mask) * width_2, width_2, axis=1)
+        if mask:
+            part = lax.ppermute(part, ("pair", "batch"), [(d, d ^ mask) for d in range(ways)])
+        full = lax.dynamic_update_slice_in_dim(full, part, (here ^ mask) * height, axis=0)
+    blocks = full
     groups = lax.axis_size("pair") * lax.axis_size("batch")
     width = blocks.shape[1]
     out_rows = blocks.shape[0] // (2 * groups)

time: 260 us -> 250 us (0.962)
  waiting for transfers between devices: 170 us -> 162 us
  other arithmetic: 12.8 us -> 9.41 us
    all_to_all x1 -> x0, waiting for transfers between devices: 26.5 us -> none  [on_device(): lax.all_to_all(features, ('pair', 'batch'), split_axis=1, concat_axis=0,...]
    ppermute x0 -> x7, waiting for transfers between devices: none -> 22.2 us  [on_device(): lax.ppermute(part, ('pair', 'batch'), [(d, d ^ mask) for d in range(ways)])]
    ppermute x0 -> x7, starting transfers between devices: none -> 5.1 us  [on_device(): lax.ppermute(part, ('pair', 'batch'), [(d, d ^ mask) for d in range(ways)])]
    all_to_all x1 -> x0, starting transfers between devices: 4.29 us -> none  [on_device(): lax.all_to_all(features, ('pair', 'batch'), split_axis=1, concat_axis=0,...]
    dynamic_update_slice x0 -> x7, local copies, waits for them, and re-layouts: none -> 3 us  [on_device(): lax.dynamic_update_slice_in_dim(full, part, (here ^ mask) * height, axis=0)]
  transfers between devices with their start and end apart: 6 -> 12, of which waited for: 6 -> 10; matrix products, arithmetic and copies ran while one was open for 5% -> 6% of each run, Pallas kernels for 0% -> 0%
where the time goes in v1:
time: 250 us
  waiting for transfers between devices  162 us (65%)
  matrix products  26.4 us (11%)
  blocking collectives  23.5 us (9%)
  between operations  13.9 us (6%)
  other arithmetic  9.41 us (4%)
  local copies, waits for them, and re-layouts  9.37 us (4%)
  starting transfers between devices  5.62 us (2%)
    reduce_scatter x2, waiting for transfers between devices, on_device(): lax.psum_scatter(kept + got, 'batch', scatter_dimension=0, tiled=True)  72.5 us
    all_gather x1, waiting for transfers between devices, on_device(): gathered = lax.all_gather(packed, 'vocab', axis=1, tiled=True)  52.4 us
    all_gather x1, blocking collectives, on_device(): every = lax.all_gather(stats, 'vocab', axis=0)  23.5 us
    ppermute x7, waiting for transfers between devices, on_device(): lax.ppermute(part, ('pair', 'batch'), [(d, d ^ mask) for d in range(ways)])  22.2 us
    dot_general x2, matrix products, on_device(): kept = jnp.dot(mine, w, preferred_element_type=jnp.float32)  14.6 us
    ppermute x2, waiting for transfers between devices, on_device(): got = lax.ppermute(sent, 'pair', [(0, 1), (1, 0)])  14.5 us
    dot_general x2, matrix products, on_device(): sent = jnp.dot(theirs, w, preferred_element_type=jnp.float32)  11.8 us
    ppermute x7, starting transfers between devices, on_device(): lax.ppermute(part, ('pair', 'batch'), [(d, d ^ mask) for d in range(ways)])  5.1 us
  transfers between devices with their start and end apart: 12, of which 10 were waited for; matrix products, arithmetic and copies ran while one was open for 6% of the time, Pallas kernels for 0%

profile of v1, /device:TPU:0, one launch (start us, length us, event | category | flops | bytes accessed | tf_op | source)
XLA Modules:
  0.0 249.9 jit_solution(16257593682243095611)
XLA Ops:
  7.2 0.0 all-gather.4.cloned.1.call-start
  7.2 0.7 broadcast_in_dim.7
  7.9 0.1 pad.6.clone
  8.0 1.7 maximum_maximum_fusion
  9.6 0.0 all-gather.4.cloned.1.call-update
  9.7 0.0 reduce-scatter.3.cloned.1.call-start
  9.8 52.4 %all-gather.4.cloned.1.call-done = bf16[144,8192]{1,0:T(8,128)(2,1)} async-done(((bf16[144,512]{1,0:T(8,128)(2,1)}), bf16[144,8192]{1,0:T(8,128)(2,1)}) %all-gather.4.cloned.1.call-update) | async-done | bytes 2359312 | tf_op jit(solution)/shard_map/all_gather | solution.py:16
  62.2 2.1 fusion
  64.3 0.9 slice_convert_fusion
  65.2 2.2 fusion.2
  67.4 0.3 broadcast_in_dim.6
  67.6 1.0 constant_dynamic-slice_fusion
  68.6 1.5 collective-permute-start
  70.1 2.7 %collective-permute-start.1 = (bf16[128,1024]{1,0:T(8,128)(2,1)}, bf16[128,1024]{1,0:T(8,128)(2,1)}, u32[]{:S(2)}, u32[]{:S(2)}) collective-permute-start(bf16[128,1024]{1,0:T(8,128)(2,1)} %get-tuple-element.13), channel_id=1, source_target_pairs={{0,32},{16,48},{32,0},{48,16},{64,96},{80,112},{96,64},{112,80},{1... | collective-permute-start | bytes 786440 | tf_op jit(solution)/shard_map/ppermute | solution.py:32
  72.8 0.5 collective-permute-start.2
  73.3 0.0 collective-permute-start.3
  73.3 0.4 collective-permute-start.4
  73.7 4.5 %collective-permute-done = bf16[128,1024]{1,0:T(8,128)(2,1)} collective-permute-done((bf16[128,1024]{1,0:T(8,128)(2,1)}, bf16[128,1024]{1,0:T(8,128)(2,1)}, u32[]{:S(2)}, u32[]{:S(2)}) %collective-permute-start) | collective-permute-done | bytes 262176 | tf_op jit(solution)/shard_map/ppermute | solution.py:32
  78.2 0.0 collective-permute-start.5
  78.2 1.0 constant_dynamic-update-slice_fusion.8
  79.2 6.9 %collective-permute-done.1 = bf16[128,1024]{1,0:T(8,128)(2,1)} collective-permute-done((bf16[128,1024]{1,0:T(8,128)(2,1)}, bf16[128,1024]{1,0:T(8,128)(2,1)}, u32[]{:S(2)}, u32[]{:S(2)}) %collective-permute-start.1) | collective-permute-done | bytes 262176 | tf_op jit(solution)/shard_map/ppermute | solution.py:32
  86.0 1.0 constant_dynamic-update-slice_fusion.7
  87.0 0.0 collective-permute-done.2
  87.0 1.0 constant_dynamic-update-slice_fusion.6
  88.0 0.3 collective-permute-done.4
  88.4 4.7 %collective-permute-done.5 = bf16[128,1024]{1,0:T(8,128)(2,1)S(1)} collective-permute-done((bf16[128,1024]{1,0:T(8,128)(2,1)S(1)}, bf16[128,1024]{1,0:T(8,128)(2,1)S(1)}, u32[]{:S(2)}, u32[]{:S(2)}) %collective-permute-start.5) | collective-permute-done | bytes 262176 | tf_op jit(solution)/shard_map/ppermute | solution.py:32
  93.2 5.8 %collective-permute-done.6 = bf16[128,1024]{1,0:T(8,128)(2,1)S(1)} collective-permute-done((bf16[128,1024]{1,0:T(8,128)(2,1)S(1)}, bf16[128,1024]{1,0:T(8,128)(2,1)S(1)}, u32[]{:S(2)}, u32[]{:S(2)}) %collective-permute-start.6) | collective-permute-done | bytes 262176 | tf_op jit(solution)/shard_map/ppermute | solution.py:32
  99.0 0.2 copy.12
  99.3 7.2 %fusion.7 = f32[512,2048]{1,0:T(8,128)} fusion(bf16[1024,4096]{1,0:T(8,128)(2,1)} %param.5, bf16[1024,1024]{1,0:T(8,128)(2,1)S(1)} %bitcast.21, s32[]{:T(128)S(6)} %select_n.71), kind=kOutput, calls=%fused_computation.9 | convolution fusion | flops 2147483648 | bytes 9437188 | tf_op jit(solution)/shard_map/dot_general | solution.py:48
  106.5 0.0 collective-permute-start.7
  106.5 7.5 %collective-permute-done.7 = f32[512,2048]{1,0:T(8,128)} collective-permute-done((f32[512,2048]{1,0:T(8,128)}, f32[512,2048]{1,0:T(8,128)}, u32[]{:S(2)}, u32[]{:S(2)}) %collective-permute-start.7) | collective-permute-done | bytes 4194336 | tf_op jit(solution)/shard_map/ppermute | solution.py:49
  114.0 8.0 %fusion.11 = f32[512,2048]{1,0:T(8,128)} fusion(f32[512,2048]{1,0:T(8,128)} %collective-permute-done.7, bf16[1024,4096]{1,0:T(8,128)(2,1)} %param.5, bf16[1024,1024]{1,0:T(8,128)(2,1)} %bitcast.22, s32[]{:T(128)S(6)} %select_n.70), kind=kOutput, calls=%fused_computation.13 | convolution fusion | flops 2148532224 | bytes 13631492 | tf_op jit(solution)/shard_map/dot_general | solution.py:50
  122.0 0.0 reduce-scatter.3.cloned.1.call-update
  122.1 0.0 reduce-scatter.5.cloned.1.call-start
  122.1 1.5 copy-done.1
  123.6 4.5 %fusion.3 = f32[512,2048]{1,0:T(8,128)S(1)} fusion(bf16[1024,4096]{1,0:T(8,128)(2,1)} %param.5, bf16[1024,1024]{1,0:T(8,128)(2,1)S(1)} %bitcast.23, s32[]{:T(128)S(6)} %select_n.71), kind=kOutput, calls=%fused_computation.5 | convolution fusion | flops 2147483648 | bytes 9437188 | tf_op jit(solution)/shard_map/dot_general | solution.py:48
  128.2 0.4 collective-permute-start.8
  128.6 7.0 %collective-permute-done.8 = f32[512,2048]{1,0:T(8,128)S(1)} collective-permute-done((f32[512,2048]{1,0:T(8,128)S(1)}, f32[512,2048]{1,0:T(8,128)S(1)}, u32[]{:S(2)}, u32[]{:S(2)}) %collective-permute-start.8) | collective-permute-done | bytes 4194336 | tf_op jit(solution)/shard_map/ppermute | solution.py:49
  135.6 6.6 %fusion.14 = f32[512,2048]{1,0:T(8,128)} fusion(f32[512,2048]{1,0:T(8,128)S(1)} %collective-permute-done.8, bf16[1024,4096]{1,0:T(8,128)(2,1)} %param.5, bf16[1024,1024]{1,0:T(8,128)(2,1)S(1)} %bitcast.24, s32[]{:T(128)S(6)} %select_n.70), kind=kOutput, calls=%fused_computation.14 | convolution fusion | flops 2148532224 | bytes 13631492 | tf_op jit(solution)/shard_map/dot_general | solution.py:50
  142.1 0.0 reduce-scatter.5.cloned.1.call-update
  142.2 24.7 %reduce-scatter.3.cloned.1.call-done = f32[128,2048]{1,0:T(8,128)} async-done(((f32[512,2048]{1,0:T(8,128)}), f32[128,2048]{1,0:T(8,128)}) %reduce-scatter.3.cloned.1.call-update) | async-done | bytes 1048592 | tf_op jit(solution)/shard_map/reduce_scatter | solution.py:51
  166.8 1.3 constant_dynamic-update-slice_fusion.1
  168.1 47.8 %reduce-scatter.5.cloned.1.call-done = f32[128,2048]{1,0:T(8,128)} async-done(((f32[512,2048]{1,0:T(8,128)}), f32[128,2048]{1,0:T(8,128)}) %reduce-scatter.5.cloned.1.call-update) | async-done | bytes 1048592 | tf_op jit(solution)/shard_map/reduce_scatter | solution.py:51
  216.0 1.3 constant_dynamic-update-slice_fusion
  217.3 0.3 slice_reduce_fusion
  217.6 0.5 exponential_reduce_fusion.1
  218.1 23.5 %all-gather.1 = f32[16,4,64]{2,1,0:T(4,128)S(1)} all-gather(f32[1,4,64]{2,1,0:T(4,128)S(1)} %maximum_bitcast_fusion), channel_id=2, replica_groups=mesh['pair'=2,'batch'=4,'vocab'=16] {'vocab'}, dimensions={0}, use_global_device_ids=true | all-gather | bytes 17408 | tf_op jit(solution)/shard_map/all_gather | solution.py:61
  241.7 1.6 slice_subtract_fusion
  (17 shorter events, 0.2 us)
Async XLA Ops:
  7.2 55.0 %all-gather.4.cloned.1.call-start = ((), (), s32[]{:S(2)}) async-start(), calls=%async_computation.2 | async-start | bytes 2506752 | tf_op jit(solution)/shard_map/all_gather | solution.py:16
  9.7 157.2 %reduce-scatter.3.cloned.1.call-start = ((), (), s32[]{:S(2)}) async-start(), calls=%async_computation.3 | async-start | bytes 5242880 | tf_op jit(solution)/shard_map/reduce_scatter | solution.py:51
  68.6 9.6 %collective-permute-start = (bf16[128,1024]{1,0:T(8,128)(2,1)}, bf16[128,1024]{1,0:T(8,128)(2,1)}, u32[]{:S(2)}, u32[]{:S(2)}) collective-permute-start(bf16[128,1024]{1,0:T(8,128)(2,1)} %get-tuple-element.14), channel_id=1, source_target_pairs={{0,16},{16,0},{32,48},{48,32},{64,80},{80,64},{96,112},{112,96},{1... | collective-permute-start | bytes 786440 | tf_op jit(solution)/shard_map/ppermute | solution.py:32
  70.1 15.9 %collective-permute-start.1 = (bf16[128,1024]{1,0:T(8,128)(2,1)}, bf16[128,1024]{1,0:T(8,128)(2,1)}, u32[]{:S(2)}, u32[]{:S(2)}) collective-permute-start(bf16[128,1024]{1,0:T(8,128)(2,1)} %get-tuple-element.13), channel_id=1, source_target_pairs={{0,32},{16,48},{32,0},{48,16},{64,96},{80,112},{96,64},{112,80},{1... | collective-permute-start | bytes 786440 | tf_op jit(solution)/shard_map/ppermute | solution.py:32
  72.8 14.2 %collective-permute-start.2 = (bf16[128,1024]{1,0:T(8,128)(2,1)S(1)}, bf16[128,1024]{1,0:T(8,128)(2,1)}, u32[]{:S(2)}, u32[]{:S(2)}) collective-permute-start(bf16[128,1024]{1,0:T(8,128)(2,1)S(1)} %get-tuple-element.12), channel_id=1, source_target_pairs={{0,48},{16,32},{32,16},{48,0},{64,112},{80,96},{96,80},{112,64},{1... | collective-permute-start | bytes 786440 | tf_op jit(solution)/shard_map/ppermute | solution.py:32
  73.3 14.7 %collective-permute-start.3 = (bf16[128,1024]{1,0:T(8,128)(2,1)S(1)}, bf16[128,1024]{1,0:T(8,128)(2,1)S(1)}, u32[]{:S(2)}, u32[]{:S(2)}) collective-permute-start(bf16[128,1024]{1,0:T(8,128)(2,1)S(1)} %get-tuple-element.11), channel_id=1, source_target_pairs={{0,64},{16,80},{32,96},{48,112},{64,0},{80,16},{96,32},{112,48},{1... | collective-permute-start | bytes 786440 | tf_op jit(solution)/shard_map/ppermute | solution.py:32
  73.3 15.0 %collective-permute-start.4 = (bf16[128,1024]{1,0:T(8,128)(2,1)S(1)}, bf16[128,1024]{1,0:T(8,128)(2,1)S(1)}, u32[]{:S(2)}, u32[]{:S(2)}) collective-permute-start(bf16[128,1024]{1,0:T(8,128)(2,1)S(1)} %get-tuple-element.10), channel_id=1, source_target_pairs={{0,80},{16,64},{32,112},{48,96},{64,16},{80,0},{96,48},{112,32},{1... | collective-permute-start | bytes 786440 | tf_op jit(solution)/shard_map/ppermute | solution.py:32
  78.2 14.9 %collective-permute-start.5 = (bf16[128,1024]{1,0:T(8,128)(2,1)S(1)}, bf16[128,1024]{1,0:T(8,128)(2,1)S(1)}, u32[]{:S(2)}, u32[]{:S(2)}) collective-permute-start(bf16[128,1024]{1,0:T(8,128)(2,1)S(1)} %get-tuple-element.9), channel_id=1, source_target_pairs={{0,96},{16,112},{32,64},{48,80},{64,32},{80,48},{96,0},{112,16},{1... | collective-permute-start | bytes 786440 | tf_op jit(solution)/shard_map/ppermute | solution.py:32
  86.0 12.9 %collective-permute-start.6 = (bf16[128,1024]{1,0:T(8,128)(2,1)S(1)}, bf16[128,1024]{1,0:T(8,128)(2,1)S(1)}, u32[]{:S(2)}, u32[]{:S(2)}) collective-permute-start(bf16[128,1024]{1,0:T(8,128)(2,1)S(1)} %get-tuple-element.8), channel_id=1, source_target_pairs={{0,112},{16,96},{32,80},{48,64},{64,48},{80,32},{96,16},{112,0},{1... | collective-permute-start | bytes 786440 | tf_op jit(solution)/shard_map/ppermute | solution.py:32
  99.2 7.2 %copy-start = (bf16[8,2,64,1024]{3,2,1,0:T(8,128)(2,1)}, bf16[8,2,64,1024]{3,2,1,0:T(8,128)(2,1)S(1)}, u32[]{:S(2)}) copy-start(bf16[8,2,64,1024]{3,2,1,0:T(8,128)(2,1)S(1)} %copy.12) | copy-start | bytes 6291460
  106.5 7.5 %collective-permute-start.7 = (f32[512,2048]{1,0:T(8,128)}, f32[512,2048]{1,0:T(8,128)}, u32[]{:S(2)}, u32[]{:S(2)}) collective-permute-start(f32[512,2048]{1,0:T(8,128)} %fusion.7), channel_id=1, source_target_pairs={{0,64},{64,0},{1,65},{65,1},{2,66},{66,2},{3,67},{67,3},{4,68},{68... | collective-permute-start | bytes 12582920 | tf_op jit(solution)/shard_map/ppermute | solution.py:49
  122.0 1.6 copy-start.1
  122.1 93.9 %reduce-scatter.5.cloned.1.call-start = ((), (), s32[]{:S(2)}) async-start(), calls=%async_computation.4 | async-start | bytes 5242880 | tf_op jit(solution)/shard_map/reduce_scatter | solution.py:51
  128.2 7.4 %collective-permute-start.8 = (f32[512,2048]{1,0:T(8,128)S(1)}, f32[512,2048]{1,0:T(8,128)S(1)}, u32[]{:S(2)}, u32[]{:S(2)}) collective-permute-start(f32[512,2048]{1,0:T(8,128)S(1)} %fusion.3), channel_id=1, source_target_pairs={{0,64},{64,0},{1,65},{65,1},{2,66},{66,2},{3,67},{67,3},{4,68},{68... | collective-permute-start | bytes 12582920 | tf_op jit(solution)/shard_map/ppermute | solution.py:49
Sparse Core Ops, SparseCore 0:
  10.7 51.4 all-gather.3
  122.2 44.6 reduce-scatter.2
  169.4 46.5 reduce-scatter.4
